TPU v7x, 128 devices: a whole 4x4x4 slice. The times are simulated.
128 devices in a mesh: rep: 4 (over z_lo, core), ep: 32 (over y, x, z_hi).
Axes of the slice: x: 4, y: 4, z: 4 (z_hi: 2, z_lo: 2; z = z_hi * 2 + z_lo), core: 2. Of those that a mesh axis runs over, the one named last changes fastest.
Arguments:
- tokens: bfloat16 [16384, 2048], P(('rep', 'ep')), may hold values from -6 to 6
- expert_ids: int32 [16384, 8], P(('rep', 'ep')), may hold values from 0 to 127, as said below
- route_weight: float32 [16384, 8], P(('rep', 'ep')), may hold values from 0.05 to 1
- hot_plan: int32 [32], replicated, may hold values from 0 to 3, as said below
- gate_proj: bfloat16 [128, 2048, 768], P(('rep', 'ep')), may hold values from -0.125 to 0.125
- up_proj: bfloat16 [128, 2048, 768], P(('rep', 'ep')), may hold values from -0.125 to 0.125
- down_proj: bfloat16 [128, 768, 2048], P(('rep', 'ep')), may hold values from -0.21875 to 0.21875
Outputs:
- layer_out: bfloat16 [16384, 2048], P(('rep', 'ep'))
- served_load: float32 [128], replicated
Inputs may be any that keep to these rules, and one draw needn't show every extreme that they name: `expert_ids`: within the rows of one device (aligned blocks of 128 tokens) a hot expert is named at most 16 times and any other expert at most 6 times. Some expert that is not hot is named exactly 6 times in every block, and the hot expert of some column exactly 16 times in every block. Expert hot_plan[c] * 32 + c is the hot expert of column c.
All inputs are finite; a program needn't handle non-finite values.
Results may differ from a plain program's by a relative error of at most 0.0057.
Values may be sent and summed in bfloat16 or wider, within the bound.
No kernel may reach another device: no remote copies, remote signals or barrier semaphores. Data moves between devices by JAX's collectives and lax.ppermute only.
A program may use at most 128 MiB of HBM per device.

v0:
```python
import jax
import jax.numpy as jnp
from jax import lax
from jax.sharding import PartitionSpec as P


def from_root(array, axis, root):
    mine = lax.axis_index(axis) == root
    return lax.psum(jnp.where(mine, array, jnp.zeros_like(array)), axis)


def expert_ffn(slot_rows, gate_mat, up_mat, down_mat):
    layout = slot_rows.shape
    flattened = slot_rows.reshape(-1, layout[-1])
    gate_in = jnp.dot(flattened, gate_mat, preferred_element_type=jnp.float32)
    up_in = jnp.dot(flattened, up_mat, preferred_element_type=jnp.float32)
    hidden = (jax.nn.silu(gate_in) * up_in).astype(jnp.bfloat16)
    result = jnp.dot(hidden, down_mat, preferred_element_type=jnp.float32).astype(jnp.bfloat16)
    return result.reshape(layout)


def local(tokens, expert_ids, route_weight, hot_plan, gate_proj, up_proj, down_proj):
    n_rep = lax.axis_size("rep")
    n_ep = lax.axis_size("ep")
    devices = n_rep * n_ep
    my_row = lax.axis_index("rep")
    my_col = lax.axis_index("ep")
    tok_rows, top_count = expert_ids.shape
    model_width = tokens.shape[1]
    routed = tok_rows * top_count
    cool_cap = max(2, 3 * routed // (4 * devices))
    hot_cap = max(4, 2 * routed // devices)
    flat_ids = expert_ids.reshape(-1)
    expert_range = jnp.arange(devices, dtype=jnp.int32)
    column_range = jnp.arange(n_ep, dtype=jnp.int32)
    one_hot = (flat_ids[:, None] == expert_range[None, :]).astype(jnp.int32)
    own_counts = jnp.sum(one_hot, axis=0, dtype=jnp.int32)
    row_match = (jnp.arange(n_rep, dtype=jnp.int32) == my_row)[:, None]
    placed = jnp.where(row_match, own_counts[None, :], jnp.zeros_like(own_counts)[None, :])
    row_counts = lax.psum(placed, ("rep", "ep"))
    same_column = expert_range[:, None] % n_ep == column_range[None, :]
    same_row = expert_range[:, None] // n_ep == hot_plan[None, :]
    hot_flag = jnp.any(same_column & same_row, axis=1)
    counts = jnp.sum(row_counts, axis=0, dtype=jnp.int32)
    hot_expert = hot_plan * n_ep + column_range
    copy_rows = row_counts[:, hot_expert].reshape(-1)
    served = jnp.where(hot_flag, jnp.zeros_like(counts), counts) + copy_rows
    served_load = served.astype(jnp.float32) / jnp.float32(routed)
    is_hot = jnp.sum(one_hot * hot_flag.astype(jnp.int32)[None, :], axis=1, dtype=jnp.int32) > 0
    ordinal = jnp.sum((jnp.cumsum(one_hot, axis=0) - 1) * one_hot, axis=1)
    home_col = flat_ids % n_ep
    source = jnp.arange(routed, dtype=jnp.int32) // top_count

    def pack_rows(slot, total):
        owners = jnp.zeros((total + 1,), jnp.int32).at[slot].set(source)[:total]
        filled = jnp.zeros((total + 1,), jnp.bool_).at[slot].set(True)[:total]
        return jnp.where(filled[:, None], tokens[owners], jnp.zeros((), jnp.bfloat16))

    home_total = devices * cool_cap
    home_slot = jnp.where(is_hot, home_total, flat_ids * cool_cap + ordinal)
    copy_total = n_ep * hot_cap
    copy_slot = jnp.where(is_hot, home_col * hot_cap + ordinal, copy_total)
    copy_send = pack_rows(copy_slot, copy_total).reshape(n_ep, hot_cap, model_width)
    copied = (
        from_root(gate_proj[0], "rep", hot_plan[my_col]),
        from_root(up_proj[0], "rep", hot_plan[my_col]),
        from_root(down_proj[0], "rep", hot_plan[my_col]),
    )
    copy_done = expert_ffn(
        lax.all_to_all(copy_send, "ep", split_axis=0, concat_axis=0, tiled=True),
        copied[0],
        copied[1],
        copied[2],
    )
    copy_back = lax.all_to_all(copy_done, "ep", split_axis=0, concat_axis=0, tiled=True)
    copy_result = copy_back.reshape(copy_total, model_width)[jnp.minimum(copy_slot, copy_total - 1)]
    home_send = pack_rows(home_slot, home_total).reshape(devices, cool_cap, model_width)
    home_done = expert_ffn(
        lax.all_to_all(home_send, ("rep", "ep"), split_axis=0, concat_axis=0, tiled=True),
        gate_proj[0],
        up_proj[0],
        down_proj[0],
    )
    home_back = lax.all_to_all(home_done, ("rep", "ep"), split_axis=0, concat_axis=0, tiled=True)
    home_result = home_back.reshape(home_total, model_width)[jnp.minimum(home_slot, home_total - 1)]
    gathered = jnp.where(is_hot[:, None], copy_result, home_result)
    shares = route_weight / jnp.sum(route_weight, axis=1, keepdims=True)
    combined = jnp.sum(
        shares[:, :, None] * gathered.reshape(tok_rows, top_count, model_width).astype(jnp.float32),
        axis=1,
    )
    return (combined.astype(jnp.bfloat16), served_load)


def solution(mesh):
    placed = (
        P(("rep", "ep"), None),
        P(("rep", "ep"), None),
        P(("rep", "ep"), None),
        P(),
        P(("rep", "ep"), None, None),
        P(("rep", "ep"), None, None),
        P(("rep", "ep"), None, None),
    )
    return jax.shard_map(
        local, mesh=mesh, in_specs=placed, out_specs=(P(("rep", "ep"), None), P()), check_vma=False
    )
```

profile of v0, /device:TPU:1, one launch (start us, length us, event | category | flops | bytes accessed | tf_op | source)
XLA Modules:
  0.0 456.8 jit_solution(834048434750761366)
XLA Ops:
  19.4 4.3 scatter_custom_fusion.3
  23.8 4.4 gather_fusion.2
  28.1 6.3 %gather.28 = bf16[128,6,2048]{2,1,0:T(8,128)(2,1)} reshape(bf16[768,2048]{1,0:T(8,128)(2,1)} %gather_fusion.2) | data formatting | bytes 6291456 | tf_op jit(solution)/shard_map/gather | solution.py:57
  34.4 4.3 scatter_custom_fusion.2
  39.0 4.7 %broadcast_select_fusion = bf16[128,6,2048]{2,1,0:T(8,128)(2,1)} fusion(bf16[128,6,2048]{2,1,0:T(8,128)(2,1)} %gather.28, pred[128,6]{1,0:T(8,128)(4,1)S(1)} %broadcast_in_dim.123), kind=kLoop, calls=%fused_computation.11 | loop fusion | flops 1572864 | bytes 6292224 | tf_op jit(solution)/shard_map/jit(_where)/select_n | solution.py:57
  43.7 11.8 %all-to-all-start.2 = ((bf16[128,6,2048]{2,1,0:T(8,128)(2,1)}), bf16[128,6,2048]{2,1,0:T(8,128)(2,1)}, u32[]{:S(2)}, u32[]{:S(2)}) async-start(bf16[128,6,2048]{2,1,0:T(8,128)(2,1)} %broadcast_select_fusion), calls=%async_computation.2 | async-start | bytes 8388608 | tf_op jit(solution)/shard_map/all_to_all | solution.py:79
  55.6 4.5 scatter_custom_fusion.1
  60.1 4.3 scatter_custom_fusion
  68.6 39.2 %all-to-all-done.2 = bf16[128,6,2048]{2,1,0:T(8,128)(2,1)} async-done(((bf16[128,6,2048]{2,1,0:T(8,128)(2,1)}), bf16[128,6,2048]{2,1,0:T(8,128)(2,1)}, u32[]{:S(2)}, u32[]{:S(2)}) %all-to-all-start.2) | async-done | bytes 3145760 | tf_op jit(solution)/shard_map/all_to_all | solution.py:79
  107.8 7.8 %all-to-all-start = ((bf16[32,16,2048]{2,1,0:T(8,128)(2,1)}), bf16[32,16,2048]{2,1,0:T(8,128)(2,1)S(1)}, u32[]{:S(2)}, u32[]{:S(2)}) async-start(bf16[32,16,2048]{2,1,0:T(8,128)(2,1)} %broadcast_select_fusion.1), calls=%async_computation | async-start | bytes 4194304 | tf_op jit(solution)/shard_map/all_to_all | solution.py:70
  115.5 6.4 %reshape.314 = bf16[768,2048]{1,0:T(8,128)(2,1)} reshape(bf16[128,6,2048]{2,1,0:T(8,128)(2,1)} %all-to-all-done.2) | data formatting | bytes 6291456 | tf_op jit(solution)/shard_map/reshape | solution.py:14
  121.9 7.0 %fusion.1 = f32[768,768]{1,0:T(8,128)} fusion(bf16[768,2048]{1,0:T(8,128)(2,1)} %reshape.314, bf16[1,2048,768]{2,1,0:T(8,128)(2,1)} %param.12), kind=kOutput, calls=%fused_computation.15 | convolution fusion | flops 2415919104 | bytes 8650752 | tf_op jit(solution)/shard_map/dot_general | solution.py:16
  128.9 12.0 %convolution_convert_fusion = bf16[768,2048]{1,0:T(8,128)(2,1)} fusion(bf16[1,768,2048]{2,1,0:T(8,128)(2,1)} %param.13, f32[768,768]{1,0:T(8,128)} %fusion.1, bf16[768,2048]{1,0:T(8,128)(2,1)} %reshape.314, bf16[1,2048,768]{2,1,0:T(8,128)(2,1)} %param.11), kind=kOutput, calls=%fused_computation.12 | convolution fusion | flops 4836950016 | bytes 14942208 | tf_op jit(solution)/shard_map/dot_general | solution.py:18
  140.9 6.3 %reshape.315 = bf16[128,6,2048]{2,1,0:T(8,128)(2,1)} reshape(bf16[768,2048]{1,0:T(8,128)(2,1)} %convolution_convert_fusion) | data formatting | bytes 6291456 | tf_op jit(solution)/shard_map/reshape | solution.py:19
  147.2 10.1 %all-to-all-start.3 = ((bf16[128,6,2048]{2,1,0:T(8,128)(2,1)}), bf16[128,6,2048]{2,1,0:T(8,128)(2,1)}, u32[]{:S(2)}, u32[]{:S(2)}) async-start(bf16[128,6,2048]{2,1,0:T(8,128)(2,1)} %reshape.315), calls=%async_computation.3 | async-start | bytes 8388608 | tf_op jit(solution)/shard_map/all_to_all | solution.py:84
  157.3 153.7 %all-reduce.3.cloned.1.call-done = (bf16[768,2048]{1,0:T(8,128)(2,1)}, bf16[2048,768]{1,0:T(8,128)(2,1)}, bf16[2048,768]{1,0:T(8,128)(2,1)}) async-done(((bf16[768,2048]{1,0:T(8,128)(2,1)}, bf16[2048,768]{1,0:T(8,128)(2,1)}, bf16[2048,768]{1,0:T(8,128)(2,1)}), (bf16[768,2048]{1,0:T(8,128)(2,1)}, bf16[2048,768]{1,0:T(8,128)(2,1)}, bf16[2048,768]{1,0:T(8,128)(2,1)})) %all-reduce.3.cloned.1.call-update) | async-done | bytes 9437200 | tf_op jit(solution)/shard_map/psum | solution.py:9
  311.0 4.8 %fusion.31 = f32[512,768]{1,0:T(8,128)} fusion(bf16[512,2048]{1,0:T(8,128)(2,1)S(1)} %bitcast.52, bf16[2048,768]{1,0:T(8,128)(2,1)} %get-tuple-element.6), kind=kOutput, calls=%fused_computation.86 | convolution fusion | flops 1610612736 | bytes 6815744 | tf_op jit(solution)/shard_map/dot_general | solution.py:15
  315.8 8.6 %convolution_convert_fusion.1 = bf16[512,2048]{1,0:T(8,128)(2,1)} fusion(bf16[768,2048]{1,0:T(8,128)(2,1)} %get-tuple-element.5, f32[512,768]{1,0:T(8,128)} %fusion.31, bf16[512,2048]{1,0:T(8,128)(2,1)S(1)} %bitcast.53, bf16[2048,768]{1,0:T(8,128)(2,1)} %get-tuple-element.7), kind=kOutput, calls=%fused_computation.21 | convolution fusion | flops 3224633344 | bytes 12058624 | tf_op jit(solution)/shard_map/dot_general | solution.py:18
  324.4 9.5 %all-to-all-start.1 = ((bf16[32,16,2048]{2,1,0:T(8,128)(2,1)}), bf16[32,16,2048]{2,1,0:T(8,128)(2,1)S(1)}, u32[]{:S(2)}, u32[]{:S(2)}) async-start(bf16[32,16,2048]{2,1,0:T(8,128)(2,1)} %bitcast.51), calls=%async_computation.1 | async-start | bytes 4194304 | tf_op jit(solution)/shard_map/all_to_all | solution.py:75
  334.3 83.8 %psum.31 = s32[4,128]{0,1:T(8,128)S(1)} all-reduce(s32[4,128]{0,1:T(8,128)S(1)} %broadcast_select_fusion.2), channel_id=1, replica_groups=mesh['rep'=4,'ep'=32] {'rep','ep'}, use_global_device_ids=true, to_apply=%region_15.16 | all-reduce | flops 512 | bytes 4096 | tf_op jit(solution)/shard_map/psum | solution.py:40
  419.5 6.3 %reshape.316 = bf16[768,2048]{1,0:T(8,128)(2,1)} reshape(bf16[128,6,2048]{2,1,0:T(8,128)(2,1)} %all-to-all-done.3) | data formatting | bytes 6291456 | tf_op jit(solution)/shard_map/reshape | solution.py:85
  425.8 11.1 %gather_fusion.3 = bf16[1024,2048]{1,0:T(8,128)(2,1)} fusion(bf16[768,2048]{1,0:T(8,128)(2,1)} %reshape.316, s32[1024]{0:T(1024)S(1)} %broadcast_clamp_fusion), kind=kCustom, calls=%fused_computation.3 | custom fusion | bytes 8392704 | tf_op jit(solution)/shard_map/gather | solution.py:85
  437.0 6.0 %gather_fusion.1 = bf16[1024,2048]{1,0:T(8,128)(2,1)} fusion(bf16[512,2048]{1,0:T(8,128)(2,1)S(1)} %bitcast.49, s32[1024]{0:T(1024)S(1)} %broadcast_clamp_fusion.1), kind=kCustom, calls=%fused_computation.1 | custom fusion | bytes 8392704 | tf_op jit(solution)/shard_map/gather | solution.py:76
  443.0 7.0 %multiply_reduce_fusion = bf16[128,2048]{1,0:T(8,128)(2,1)} fusion(bf16[1024,2048]{1,0:T(8,128)(2,1)} %gather_fusion.3, bf16[1024,2048]{1,0:T(8,128)(2,1)} %gather_fusion.1, f32[128,8]{1,0:T(8,128)S(1)} %copy.18, pred[128,8]{1,0:T(8,128)(4,1)S(1)} %gt.32), kind=kLoop, calls=%fused_computation.9 | loop fusion | flops 8126464 | bytes 8918016 | tf_op jit(solution)/shard_map/reduce_sum | solution.py:88
  (67 shorter events, 17.5 us)
Async XLA Ops:
  7.2 16.6 %copy-start = (bf16[128,2048]{1,0:T(8,128)(2,1)S(1)}, bf16[128,2048]{1,0:T(8,128)(2,1)}, u32[]{:S(2)}) copy-start(bf16[128,2048]{1,0:T(8,128)(2,1)} %param.7) | copy-start | bytes 1572868
  7.2 303.8 %all-reduce.3.cloned.1.call-start = ((), (), s32[]{:S(2)}) async-start(), calls=%async_computation.4 | async-start | bytes 18874368 | tf_op jit(solution)/shard_map/psum | solution.py:9
  9.2 3.9 copy-start.2
  9.2 4.9 %copy-start.3 = (bf16[1,2048,768]{2,1,0:T(8,128)(2,1)S(1)}, bf16[1,2048,768]{2,1,0:T(8,128)(2,1)}, u32[]{:S(2)}) copy-start(bf16[1,2048,768]{2,1,0:T(8,128)(2,1)} %param.11) | copy-start | bytes 9437188
  17.1 0.7 copy-start.5
  17.1 1.6 copy-start.6
  43.7 64.1 %all-to-all-start.2 = ((bf16[128,6,2048]{2,1,0:T(8,128)(2,1)}), bf16[128,6,2048]{2,1,0:T(8,128)(2,1)}, u32[]{:S(2)}, u32[]{:S(2)}) async-start(bf16[128,6,2048]{2,1,0:T(8,128)(2,1)} %broadcast_select_fusion), calls=%async_computation.2 | async-start | bytes 8388608 | tf_op jit(solution)/shard_map/all_to_all | solution.py:79
  107.8 39.4 %all-to-all-start = ((bf16[32,16,2048]{2,1,0:T(8,128)(2,1)}), bf16[32,16,2048]{2,1,0:T(8,128)(2,1)S(1)}, u32[]{:S(2)}, u32[]{:S(2)}) async-start(bf16[32,16,2048]{2,1,0:T(8,128)(2,1)} %broadcast_select_fusion.1), calls=%async_computation | async-start | bytes 4194304 | tf_op jit(solution)/shard_map/all_to_all | solution.py:70
  147.2 177.3 %all-to-all-start.3 = ((bf16[128,6,2048]{2,1,0:T(8,128)(2,1)}), bf16[128,6,2048]{2,1,0:T(8,128)(2,1)}, u32[]{:S(2)}, u32[]{:S(2)}) async-start(bf16[128,6,2048]{2,1,0:T(8,128)(2,1)} %reshape.315), calls=%async_computation.3 | async-start | bytes 8388608 | tf_op jit(solution)/shard_map/all_to_all | solution.py:84
  324.4 9.6 %copy-start.4 = (f32[128,8]{0,1:T(8,128)S(1)}, f32[128,8]{0,1:T(8,128)}, u32[]{:S(2)}) copy-start(f32[128,8]{0,1:T(8,128)} %param.9) | copy-start | bytes 12292
  324.4 112.5 %all-to-all-start.1 = ((bf16[32,16,2048]{2,1,0:T(8,128)(2,1)}), bf16[32,16,2048]{2,1,0:T(8,128)(2,1)S(1)}, u32[]{:S(2)}, u32[]{:S(2)}) async-start(bf16[32,16,2048]{2,1,0:T(8,128)(2,1)} %bitcast.51), calls=%async_computation.1 | async-start | bytes 4194304 | tf_op jit(solution)/shard_map/all_to_all | solution.py:75
  436.9 13.0 %copy-start.1 = (bf16[128,2048]{1,0:T(8,128)(2,1)S(1)}, bf16[128,2048]{1,0:T(8,128)(2,1)}, u32[]{:S(2)}) copy-start(bf16[128,2048]{1,0:T(8,128)(2,1)} %param.7) | copy-start | bytes 1572868
Sparse Core Ops, SparseCore 0:
  17.3 293.6 all-reduce.2
where the time goes:
time: 458 us; the launch traced here: 457 us
  waiting for transfers between devices  193 us (42%)
  blocking collectives  83.8 us (18%)
  local copies, waits for them, and re-layouts  71.5 us (16%)
  starting transfers between devices  39.2 us (9%)
  matrix products  32.5 us (7%)
  other arithmetic  21.9 us (5%)
  between operations  15 us (3%)
    psum x1, waiting for transfers between devices, from_root(): return lax.psum(jnp.where(mine, array, jnp.zeros_like(array)), axis)  154 us
    psum x1, blocking collectives, local(): row_counts = lax.psum(placed, ('rep', 'ep'))  83.8 us
    all_to_all x1, waiting for transfers between devices, local(): lax.all_to_all(home_send, ('rep', 'ep'), split_axis=0, concat_axis=0, til...  39.2 us
    dot_general x2, matrix products, expert_ffn(): jnp.dot(hidden, down_mat, preferred_element_type=jnp.float32)  20.7 us
    gather x3, local copies, waits for them, and re-layouts, pack_rows(): tokens[owners]  13.1 us
    all_to_all x1, starting transfers between devices, local(): lax.all_to_all(home_send, ('rep', 'ep'), split_axis=0, concat_axis=0, til...  11.8 us
    gather x1, local copies, waits for them, and re-layouts, local(): home_back.reshape(home_total, model_width)  11.1 us
    all_to_all x1, starting transfers between devices, local(): lax.all_to_all(home_done, ('rep', 'ep'), split_axis=0, concat_axis=0, til...  10.1 us
  transfers between devices with their start and end apart: 5, of which 2 were waited for; matrix products, arithmetic and copies ran while one was open for 23% of the time, Pallas kernels for 0%

commit v1 on v0

--- a/solution.py
+++ b/solution.py
@@ -4,9 +4,14 @@
 from jax.sharding import PartitionSpec as P
 
 
+def _state_skins(shard_in, axis_name):
+    y2 = jnp.sum(jax.lax.all_gather(shard_in, axis_name), 0)
+    return y2
+
+
 def from_root(array, axis, root):
     mine = lax.axis_index(axis) == root
-    return lax.psum(jnp.where(mine, array, jnp.zeros_like(array)), axis)
+    return _state_skins(jnp.where(mine, array, jnp.zeros_like(array)), axis)
 
 
 def expert_ffn(slot_rows, gate_mat, up_mat, down_mat):

time: 458 us -> 652 us (1.42); the launches traced: 457 us -> 643 us
  waiting for transfers between devices: 193 us -> 345 us
  other arithmetic: 21.9 us -> 54.8 us
    all_gather x0 -> x3, waiting for transfers between devices: none -> 306 us  [_state_skins(): y2 = jnp.sum(jax.lax.all_gather(shard_in, axis_name), 0)]
    psum x1 -> x0, waiting for transfers between devices: 154 us -> none  [from_root(): return lax.psum(jnp.where(mine, array, jnp.zeros_like(array)), axis)]
    reduce_sum x0 -> x3, other arithmetic: none -> 28.3 us  [_state_skins(): y2 = jnp.sum(jax.lax.all_gather(shard_in, axis_name), 0)]
  transfers between devices with their start and end apart: 5 -> 7, of which waited for: 2 -> 4; matrix products, arithmetic and copies ran while one was open for 23% -> 22% of each run, Pallas kernels for 0% -> 0%
where the time goes in v1:
time: 652 us; the launch traced here: 643 us
  waiting for transfers between devices  345 us (53%)
  blocking collectives  85.8 us (13%)
  local copies, waits for them, and re-layouts  70.7 us (11%)
  other arithmetic  54.8 us (8%)
  starting transfers between devices  39 us (6%)
  matrix products  32.5 us (5%)
  between operations  14.9 us (2%)
    all_gather x3, waiting for transfers between devices, _state_skins(): y2 = jnp.sum(jax.lax.all_gather(shard_in, axis_name), 0)  306 us
    psum x1, blocking collectives, local(): row_counts = lax.psum(placed, ('rep', 'ep'))  85.8 us
    all_to_all x1, waiting for transfers between devices, local(): lax.all_to_all(home_send, ('rep', 'ep'), split_axis=0, concat_axis=0, til...  39 us
    reduce_sum x3, other arithmetic, _state_skins(): y2 = jnp.sum(jax.lax.all_gather(shard_in, axis_name), 0)  28.3 us
    dot_general x2, matrix products, expert_ffn(): jnp.dot(hidden, down_mat, preferred_element_type=jnp.float32)  20.8 us
    gather x3, local copies, waits for them, and re-layouts, pack_rows(): tokens[owners]  13.1 us
  transfers between devices with their start and end apart: 7, of which 4 were waited for; matrix products, arithmetic and copies ran while one was open for 22% of the time, Pallas kernels for 0%

profile of v1, /device:TPU:1, one launch (start us, length us, event | category | flops | bytes accessed | tf_op | source)
XLA Modules:
  0.0 642.9 jit_solution(2075141681361748877)
XLA Ops:
  31.7 6.3 gather.28
  47.3 11.7 %all-to-all-start.2 = ((bf16[128,6,2048]{2,1,0:T(8,128)(2,1)}), bf16[128,6,2048]{2,1,0:T(8,128)(2,1)}, u32[]{:S(2)}, u32[]{:S(2)}) async-start(bf16[128,6,2048]{2,1,0:T(8,128)(2,1)} %broadcast_select_fusion), calls=%async_computation.2 | async-start | bytes 8388608 | tf_op jit(solution)/shard_map/all_to_all | solution.py:84
  59.0 4.8 scatter_custom_fusion.1
  72.3 39.0 %all-to-all-done.2 = bf16[128,6,2048]{2,1,0:T(8,128)(2,1)} async-done(((bf16[128,6,2048]{2,1,0:T(8,128)(2,1)}), bf16[128,6,2048]{2,1,0:T(8,128)(2,1)}, u32[]{:S(2)}, u32[]{:S(2)}) %all-to-all-start.2) | async-done | bytes 3145760 | tf_op jit(solution)/shard_map/all_to_all | solution.py:84
  111.2 7.8 %all-to-all-start = ((bf16[32,16,2048]{2,1,0:T(8,128)(2,1)}), bf16[32,16,2048]{2,1,0:T(8,128)(2,1)S(1)}, u32[]{:S(2)}, u32[]{:S(2)}) async-start(bf16[32,16,2048]{2,1,0:T(8,128)(2,1)} %broadcast_select_fusion.4), calls=%async_computation | async-start | bytes 4194304 | tf_op jit(solution)/shard_map/all_to_all | solution.py:75
  119.0 6.3 reshape.314
  125.3 6.9 %fusion.1 = f32[768,768]{1,0:T(8,128)} fusion(bf16[768,2048]{1,0:T(8,128)(2,1)} %reshape.314, bf16[1,2048,768]{2,1,0:T(8,128)(2,1)} %param.12), kind=kOutput, calls=%fused_computation.14 | convolution fusion | flops 2415919104 | bytes 8650752 | tf_op jit(solution)/shard_map/dot_general | solution.py:21
  132.2 12.0 %convolution_convert_fusion = bf16[768,2048]{1,0:T(8,128)(2,1)} fusion(bf16[1,768,2048]{2,1,0:T(8,128)(2,1)} %param.13, f32[768,768]{1,0:T(8,128)} %fusion.1, bf16[768,2048]{1,0:T(8,128)(2,1)} %reshape.314, bf16[1,2048,768]{2,1,0:T(8,128)(2,1)} %param.11), kind=kOutput, calls=%fused_computation.12 | convolution fusion | flops 4836950016 | bytes 14942208 | tf_op jit(solution)/shard_map/dot_general | solution.py:23
  144.2 6.3 reshape.315
  150.4 10.2 %all-to-all-start.3 = ((bf16[128,6,2048]{2,1,0:T(8,128)(2,1)}), bf16[128,6,2048]{2,1,0:T(8,128)(2,1)}, u32[]{:S(2)}, u32[]{:S(2)}) async-start(bf16[128,6,2048]{2,1,0:T(8,128)(2,1)} %reshape.315), calls=%async_computation.3 | async-start | bytes 8388608 | tf_op jit(solution)/shard_map/all_to_all | solution.py:89
  160.7 85.5 %all-gather.4.cloned.1.call-done = bf16[4,2048,768]{2,1,0:T(8,128)(2,1)} async-done(((bf16[1,2048,768]{2,1,0:T(8,128)(2,1)}), bf16[4,2048,768]{2,1,0:T(8,128)(2,1)}) %all-gather.4.cloned.1.call-update) | async-done | bytes 12582928 | tf_op jit(solution)/shard_map/all_gather | solution.py:8
  246.2 9.0 %reduce_sum.96 = bf16[2048,768]{1,0:T(8,128)(2,1)} reduce(bf16[4,2048,768]{2,1,0:T(8,128)(2,1)} %all-gather.4.cloned.1.call-done, bf16[]{:T(256)} %constant.114.clone.1), dimensions={0}, to_apply=%region_8.9 | reduce | flops 4718592 | bytes 15728642 | tf_op jit(solution)/shard_map/reduce_sum | solution.py:8
  255.2 110.7 %all-gather.6.cloned.1.call-done = bf16[4,2048,768]{2,1,0:T(8,128)(2,1)} async-done(((bf16[1,2048,768]{2,1,0:T(8,128)(2,1)}), bf16[4,2048,768]{2,1,0:T(8,128)(2,1)}) %all-gather.6.cloned.1.call-update) | async-done | bytes 12582928 | tf_op jit(solution)/shard_map/all_gather | solution.py:8
  366.0 9.0 %reduce_sum.97 = bf16[2048,768]{1,0:T(8,128)(2,1)} reduce(bf16[4,2048,768]{2,1,0:T(8,128)(2,1)} %all-gather.6.cloned.1.call-done, bf16[]{:T(256)} %constant.114.clone.1), dimensions={0}, to_apply=%region_9.10 | reduce | flops 4718592 | bytes 15728642 | tf_op jit(solution)/shard_map/reduce_sum | solution.py:8
  375.0 109.8 %all-gather.8.cloned.1.call-done = bf16[4,768,2048]{2,1,0:T(8,128)(2,1)} async-done(((bf16[1,768,2048]{2,1,0:T(8,128)(2,1)}), bf16[4,768,2048]{2,1,0:T(8,128)(2,1)}) %all-gather.8.cloned.1.call-update) | async-done | bytes 12582928 | tf_op jit(solution)/shard_map/all_gather | solution.py:8
  484.8 10.2 %reduce_sum.98 = bf16[768,2048]{1,0:T(8,128)(2,1)} reduce(bf16[4,768,2048]{2,1,0:T(8,128)(2,1)} %all-gather.8.cloned.1.call-done, bf16[]{:T(256)} %constant.114.clone.1), dimensions={0}, to_apply=%region_10.11 | reduce | flops 4718592 | bytes 15728642 | tf_op jit(solution)/shard_map/reduce_sum | solution.py:8
  495.1 4.8 fusion.31
  499.9 8.9 %convolution_convert_fusion.1 = bf16[512,2048]{1,0:T(8,128)(2,1)} fusion(bf16[768,2048]{1,0:T(8,128)(2,1)} %reduce_sum.98, f32[512,768]{1,0:T(8,128)} %fusion.31, bf16[512,2048]{1,0:T(8,128)(2,1)S(1)} %bitcast.50, bf16[2048,768]{1,0:T(8,128)(2,1)} %reduce_sum.97), kind=kOutput, calls=%fused_computation.21 | convolution fusion | flops 3224633344 | bytes 12058624 | tf_op jit(solution)/shard_map/dot_general | solution.py:23
  508.8 9.2 %all-to-all-start.1 = ((bf16[32,16,2048]{2,1,0:T(8,128)(2,1)}), bf16[32,16,2048]{2,1,0:T(8,128)(2,1)S(1)}, u32[]{:S(2)}, u32[]{:S(2)}) async-start(bf16[32,16,2048]{2,1,0:T(8,128)(2,1)} %bitcast.48), calls=%async_computation.1 | async-start | bytes 4194304 | tf_op jit(solution)/shard_map/all_to_all | solution.py:80
  518.4 85.8 %psum.7 = s32[4,128]{0,1:T(8,128)S(1)} all-reduce(s32[4,128]{0,1:T(8,128)S(1)} %broadcast_select_fusion.5), channel_id=1, replica_groups=mesh['rep'=4,'ep'=32] {'rep','ep'}, use_global_device_ids=true, to_apply=%region_15.16 | all-reduce | flops 512 | bytes 4096 | tf_op jit(solution)/shard_map/psum | solution.py:45
  605.6 6.3 reshape.316
  611.9 11.1 %gather_fusion.3 = bf16[1024,2048]{1,0:T(8,128)(2,1)} fusion(bf16[768,2048]{1,0:T(8,128)(2,1)} %reshape.316, s32[1024]{0:T(1024)S(1)} %broadcast_clamp_fusion), kind=kCustom, calls=%fused_computation.3 | custom fusion | bytes 8392704 | tf_op jit(solution)/shard_map/gather | solution.py:90
  623.0 6.1 gather_fusion.1
  629.1 7.0 %multiply_reduce_fusion = bf16[128,2048]{1,0:T(8,128)(2,1)} fusion(bf16[1024,2048]{1,0:T(8,128)(2,1)} %gather_fusion.3, bf16[1024,2048]{1,0:T(8,128)(2,1)} %gather_fusion.1, f32[128,8]{1,0:T(8,128)S(1)} %copy.25, pred[128,8]{1,0:T(8,128)(4,1)S(1)} %gt.32), kind=kLoop, calls=%fused_computation.9 | loop fusion | flops 8126464 | bytes 8918016 | tf_op jit(solution)/shard_map/reduce_sum | solution.py:93
  (73 shorter events, 43.2 us)
Async XLA Ops:
  7.2 20.3 %copy-start = (bf16[128,2048]{1,0:T(8,128)(2,1)S(1)}, bf16[128,2048]{1,0:T(8,128)(2,1)}, u32[]{:S(2)}) copy-start(bf16[128,2048]{1,0:T(8,128)(2,1)} %param.7) | copy-start | bytes 1572868
  7.2 239.0 %all-gather.4.cloned.1.call-start = ((), (), s32[]{:S(2)}) async-start(), calls=%async_computation.4 | async-start | bytes 15728640 | tf_op jit(solution)/shard_map/all_gather | solution.py:8
  13.0 352.9 %all-gather.6.cloned.1.call-start = ((), (), s32[]{:S(2)}) async-start(), calls=%async_computation.5 | async-start | bytes 15728640 | tf_op jit(solution)/shard_map/all_gather | solution.py:8
  16.9 468.0 %all-gather.8.cloned.1.call-start = ((), (), s32[]{:S(2)}) async-start(), calls=%async_computation.6 | async-start | bytes 15728640 | tf_op jit(solution)/shard_map/all_gather | solution.py:8
  20.8 0.7 copy-start.3
  20.8 1.6 copy-start.4
  47.3 63.9 %all-to-all-start.2 = ((bf16[128,6,2048]{2,1,0:T(8,128)(2,1)}), bf16[128,6,2048]{2,1,0:T(8,128)(2,1)}, u32[]{:S(2)}, u32[]{:S(2)}) async-start(bf16[128,6,2048]{2,1,0:T(8,128)(2,1)} %broadcast_select_fusion), calls=%async_computation.2 | async-start | bytes 8388608 | tf_op jit(solution)/shard_map/all_to_all | solution.py:84
  111.2 39.2 %all-to-all-start = ((bf16[32,16,2048]{2,1,0:T(8,128)(2,1)}), bf16[32,16,2048]{2,1,0:T(8,128)(2,1)S(1)}, u32[]{:S(2)}, u32[]{:S(2)}) async-start(bf16[32,16,2048]{2,1,0:T(8,128)(2,1)} %broadcast_select_fusion.4), calls=%async_computation | async-start | bytes 4194304 | tf_op jit(solution)/shard_map/all_to_all | solution.py:75
  150.4 358.3 %all-to-all-start.3 = ((bf16[128,6,2048]{2,1,0:T(8,128)(2,1)}), bf16[128,6,2048]{2,1,0:T(8,128)(2,1)}, u32[]{:S(2)}, u32[]{:S(2)}) async-start(bf16[128,6,2048]{2,1,0:T(8,128)(2,1)} %reshape.315), calls=%async_computation.3 | async-start | bytes 8388608 | tf_op jit(solution)/shard_map/all_to_all | solution.py:89
  508.8 9.4 %copy-start.2 = (f32[128,8]{0,1:T(8,128)S(1)}, f32[128,8]{0,1:T(8,128)}, u32[]{:S(2)}) copy-start(f32[128,8]{0,1:T(8,128)} %param.9) | copy-start | bytes 12292
  508.8 114.3 %all-to-all-start.1 = ((bf16[32,16,2048]{2,1,0:T(8,128)(2,1)}), bf16[32,16,2048]{2,1,0:T(8,128)(2,1)S(1)}, u32[]{:S(2)}, u32[]{:S(2)}) async-start(bf16[32,16,2048]{2,1,0:T(8,128)(2,1)} %bitcast.48), calls=%async_computation.1 | async-start | bytes 4194304 | tf_op jit(solution)/shard_map/all_to_all | solution.py:80
  623.0 13.1 %copy-start.1 = (bf16[128,2048]{1,0:T(8,128)(2,1)S(1)}, bf16[128,2048]{1,0:T(8,128)(2,1)}, u32[]{:S(2)}) copy-start(bf16[128,2048]{1,0:T(8,128)(2,1)} %param.7) | copy-start | bytes 1572868
Sparse Core Ops, SparseCore 0:
  13.1 233.0 all-gather.3
  247.9 118.0 all-gather.5
  367.6 117.1 all-gather.7
